TPU v7x, 128 devices: a whole 4x4x4 slice. The times are simulated.
128 devices in a mesh: layer: 16 (over y, z_hi, core), feat: 8 (over x, z_lo).
Axes of the slice: x: 4, y: 4, z: 4 (z_hi: 2, z_lo: 2; z = z_hi * 2 + z_lo), core: 2. Of those that a mesh axis runs over, the one named last changes fastest.
Arguments:
- tokens_in: bfloat16 [512, 4096], P('feat', 'layer'), may hold values from -6 to 6
- targets: bfloat16 [512, 4096], P('feat', 'layer'), may hold values from -6 to 6
- enc_weight: bfloat16 [2048, 131072], P(None, ('layer', 'feat')), may hold values from -0.125 to 0.125
- enc_bias: float32 [131072], P(('layer', 'feat')), may hold values from -1 to 0.5
- dec_weight: bfloat16 [2, 131072, 2048], P(None, ('layer', 'feat')), may hold values from -0.0234375 to 0.0234375
Outputs:
- recon_error: float32 [512, 4096], P('feat', 'layer')
- mean_square: float32 [], replicated
- enc_grad: bfloat16 [2048, 131072], P(None, ('layer', 'feat'))
- bias_grad: float32 [131072], P(('layer', 'feat'))
- dec_grad: bfloat16 [2, 131072, 2048], P(None, ('layer', 'feat'))
All inputs are finite; a program needn't handle non-finite values.
Results may differ from a plain program's by a relative error of at most 0.02.
Values may be sent and summed in bfloat16 or wider, within the bound.
A program may use at most 128 MiB of HBM per device.

v0:
```python
import jax
import jax.numpy as jnp
from jax import lax
from jax.sharding import PartitionSpec as P

D = 2048
LAYERS = 2
TOK = 512
loss_scale = 64.0


def swapped(value, axis, stride):
    mask = 2**stride
    pairs = [(source, source ^ mask) for source in range(lax.axis_size(axis))]
    return lax.ppermute(value, axis, pairs)


def arrange_group(gathered, which_group, feat_count, sub_count):
    row_count = gathered.shape[1]
    col_count = gathered.shape[2]
    blocks = gathered.reshape(gathered.shape[0] // feat_count, feat_count, row_count, col_count)
    chosen = lax.dynamic_slice_in_dim(blocks, which_group * sub_count, sub_count, 0)
    return jnp.transpose(chosen, (1, 2, 0, 3)).reshape(
        feat_count * row_count, sub_count * col_count
    )


def order_pair(current, partner, member, bit_level, axis_dim):
    lower_first = member >> bit_level & 1 == 0
    leading = jnp.where(lower_first, current, partner)
    trailing = jnp.where(lower_first, partner, current)
    return jnp.concatenate([leading, trailing], axis_dim)


def on_device(tokens_in, targets, enc_weight, enc_bias, dec_weight):
    sub_count = lax.axis_size("layer") // LAYERS
    position = lax.axis_index("layer")
    layer_group = position // sub_count
    member = position % sub_count
    feat_count = lax.axis_size("feat")
    row_count = tokens_in.shape[0]
    col_count = tokens_in.shape[1]
    bit_count = sub_count.bit_length() - 1
    joined = tokens_in
    for bit_level in range(bit_count):
        partner = swapped(joined, "layer", bit_level)
        joined = order_pair(joined, partner, member, bit_level, 1)
    inputs = lax.all_gather(joined, "feat", axis=0, tiled=True)
    pre_act = jnp.dot(inputs, enc_weight, preferred_element_type=jnp.float32) + enc_bias
    features = jnp.maximum(pre_act, 0.0).astype(jnp.bfloat16)
    partial_value = jnp.einsum(
        "tf,kfd->tkd", features, dec_weight, preferred_element_type=jnp.float32
    )
    summed = lax.psum(partial_value.astype(jnp.bfloat16), "feat").astype(jnp.float32)
    summed_rows = lax.dynamic_slice_in_dim(summed, lax.axis_index("feat") * row_count, row_count, 0)
    gathered = lax.all_gather(
        summed_rows[None].astype(jnp.bfloat16), "layer", axis=0, tiled=True
    ).astype(jnp.float32)
    columns = lax.dynamic_slice_in_dim(gathered, member * col_count, col_count, 3)
    own_part = jnp.sum(
        lax.dynamic_slice_in_dim(columns, layer_group * sub_count, sub_count, 0)[:, :, 0, :], 0
    )
    prev_part = jnp.sum(
        lax.dynamic_slice_in_dim(
            columns, jnp.maximum(layer_group - 1, 0) * sub_count, sub_count, 0
        )[:, :, 1, :],
        0,
    )
    rebuilt = own_part + jnp.where(layer_group > 0, prev_part, 0.0)
    recon_error = rebuilt - targets.astype(jnp.float32)
    squares = lax.psum(jnp.sum(recon_error * recon_error), ("layer", "feat"))
    mean_square = squares / (LAYERS * TOK * D)
    scaled = (loss_scale / TOK * recon_error).astype(jnp.bfloat16)
    gathered = lax.all_gather(scaled[None], ("layer", "feat"), axis=0, tiled=True)
    own_grad = arrange_group(gathered, layer_group, feat_count, sub_count)
    next_index = jnp.minimum(layer_group + 1, LAYERS - 1)
    next_grad = arrange_group(gathered, next_index, feat_count, sub_count)
    next_grad = jnp.where(layer_group + 1 < LAYERS, next_grad, jnp.zeros_like(next_grad))
    recon_grads = jnp.stack([own_grad, next_grad], 0)
    feature_grad = jnp.einsum(
        "ktd,kfd->tf", recon_grads, dec_weight, preferred_element_type=jnp.float32
    )
    preact_grad = jnp.where(pre_act > 0.0, feature_grad, 0.0).astype(jnp.bfloat16)
    dec_grad = jnp.einsum(
        "tf,ktd->kfd", features, recon_grads, preferred_element_type=jnp.float32
    ).astype(jnp.bfloat16)
    enc_grad = lax.dot_general(
        inputs, preact_grad, (((0,), (0,)), ((), ())), preferred_element_type=jnp.float32
    ).astype(jnp.bfloat16)
    bias_grad = jnp.sum(preact_grad.astype(jnp.float32), 0)
    return (recon_error, mean_square, enc_grad, bias_grad, dec_grad)


def solution(mesh):
    placed = (
        P("feat", "layer"),
        P("feat", "layer"),
        P(None, ("layer", "feat")),
        P(("layer", "feat")),
        P(None, ("layer", "feat"), None),
    )
    return jax.shard_map(
        on_device,
        mesh=mesh,
        in_specs=placed,
        out_specs=(
            P("feat", "layer"),
            P(),
            P(None, ("layer", "feat")),
            P(("layer", "feat")),
            P(None, ("layer", "feat"), None),
        ),
        check_vma=False,
    )
```

profile of v0, /device:TPU:1, one launch (start us, length us, event | category | flops | bytes accessed | tf_op | source)
XLA Modules:
  0.0 725.6 jit_solution(8421036581591228015)
XLA Ops:
  7.2 0.0 all-gather.6.cloned.1.call-start
  7.2 1.5 collective-permute-start
  8.7 1.1 collective-permute-done
  9.7 0.8 broadcast_select_fusion.5
  10.5 3.8 collective-permute-start.1
  14.3 2.1 collective-permute-done.1
  16.5 1.4 collective-permute-start.2
  17.9 2.8 collective-permute-done.2
  20.7 0.7 pad_maximum_fusion
  21.5 0.0 all-gather.6.cloned.1.call-update
  21.5 0.0 copy-start.4
  21.5 0.0 all-reduce.2.cloned.1.call-start
  21.5 52.6 %all-gather.6.cloned.1.call-done = bf16[512,2048]{1,0:T(8,128)(2,1)} async-done(((bf16[64,2048]{1,0:T(8,128)(2,1)}), bf16[512,2048]{1,0:T(8,128)(2,1)}) %all-gather.6.cloned.1.call-update) | async-done | bytes 2097168 | tf_op jit(solution)/shard_map/all_gather | solution.py:48
  74.2 5.1 fusion.7
  79.3 0.0 copy-start.5
  79.3 1.3 copy-done.5
  80.7 0.0 copy-done.4
  80.7 9.4 %convolution_convert_fusion = bf16[512,2,2048]{2,0,1:T(8,128)(2,1)} fusion(bf16[2,1024,2048]{2,1,0:T(8,128)(2,1)} %param.9, f32[512,1024]{1,0:T(8,128)S(1)} %fusion.7, f32[1024]{0:T(1024)S(1)} %copy-done.4), kind=kOutput, calls=%fused_computation.1 | convolution fusion | flops 4298637312 | bytes 14684160 | tf_op jit(solution)/shard_map/tf,kfd->tkd/dot_general | solution.py:51
  90.1 0.0 all-reduce.2.cloned.1.call-update
  90.1 0.0 all-gather.8.cloned.1.call-start
  90.2 184.6 %all-reduce.2.cloned.1.call-done = bf16[512,2,2048]{2,0,1:T(8,128)(2,1)} async-done(((bf16[512,2,2048]{2,0,1:T(8,128)(2,1)}), bf16[512,2,2048]{2,0,1:T(8,128)(2,1)}) %all-reduce.2.cloned.1.call-update) | async-done | bytes 4194320 | tf_op jit(solution)/shard_map/psum | solution.py:54
  274.8 1.9 convert_convert_fusion
  276.7 0.0 all-gather.8.cloned.1.call-update
  276.7 0.0 all-gather.10.cloned.1.call-start
  276.8 0.0 copy-start.2
  276.9 75.4 %all-gather.8.cloned.1.call-done = bf16[1024,2,2048]{2,0,1:T(8,128)(2,1)} async-done(((bf16[64,2,2048]{2,0,1:T(8,128)(2,1)}), bf16[1024,2,2048]{2,0,1:T(8,128)(2,1)}) %all-gather.8.cloned.1.call-update) | async-done | bytes 8388624 | tf_op jit(solution)/shard_map/all_gather | solution.py:56
  352.2 11.3 %bitcast_convert_fusion = f32[16,64,2,2048]{3,1,0,2:T(8,128)} fusion(bf16[1024,2,2048]{2,0,1:T(8,128)(2,1)} %all-gather.8.cloned.1.call-done), kind=kLoop, calls=%fused_computation.30 | loop fusion | flops 4194304 | bytes 25165824 | tf_op jit(solution)/shard_map/convert_element_type | solution.py:58
  363.5 1.7 dynamic-slice_reduce_fusion
  365.2 0.0 copy-done.2
  365.2 0.6 multiply_convert_fusion
  365.9 0.0 all-gather.10.cloned.1.call-update
  365.9 0.6 multiply_reduce_fusion
  366.5 64.1 %psum.15 = f32[]{:T(128)} all-reduce(f32[]{:T(128)} %multiply_reduce_fusion), channel_id=1, replica_groups=mesh['layer'=16,'feat'=8] {'layer','feat'}, use_global_device_ids=true, to_apply=%region_4.5 | all-reduce | flops 1 | bytes 8 | tf_op jit(solution)/shard_map/psum | solution.py:71
  431.3 238.1 %all-gather.10.cloned.1.call-done = bf16[8192,256]{1,0:T(8,128)(2,1)} async-done(((bf16[64,256]{1,0:T(8,128)(2,1)}), bf16[8192,256]{1,0:T(8,128)(2,1)}) %all-gather.10.cloned.1.call-update) | async-done | bytes 4194320 | tf_op jit(solution)/shard_map/all_gather | solution.py:74
  669.4 2.7 constant_dynamic-slice_fusion
  672.1 0.0 copy-done.1
  672.1 4.4 fusion
  676.5 2.9 stack_reshape.3
  679.4 1.5 constant_dynamic-update-slice_fusion.1
  680.8 3.1 select_n.126
  683.9 0.0 slice-start
  683.9 1.5 constant_dynamic-update-slice_fusion
  685.4 11.2 %convert_bitcast_fusion = bf16[2,1024,2048]{1,2,0:T(8,128)(2,1)} fusion(bf16[2,512,2048]{2,1,0:T(8,128)(2,1)} %constant_dynamic-update-slice_fusion, f32[512,1024]{1,0:T(8,128)} %copy-done.5, f32[1024]{0:T(1024)S(1)} %copy-done.4), kind=kOutput, calls=%fused_computation | convolution fusion | flops 4300734464 | bytes 14684160 | tf_op jit(solution)/shard_map/tf,ktd->kfd/dot_general | solution.py:84
  696.6 0.0 copy-done
  696.6 5.2 convert_reduce_fusion
  701.8 11.7 %copy.13 = bf16[2,1024,2048]{2,1,0:T(8,128)(2,1)} copy(bf16[2,1024,2048]{1,2,0:T(8,128)(2,1)} %convert_bitcast_fusion) | data formatting | bytes 16777216
  713.6 0.0 copy-done.3
  713.6 4.4 convolution_convert_fusion.1
  (13 shorter events, 0.1 us)
Async XLA Ops:
  7.2 67.0 %all-gather.6.cloned.1.call-start = ((), (), s32[]{:S(2)}) async-start(), calls=%async_computation | async-start | bytes 2359296 | tf_op jit(solution)/shard_map/all_gather | solution.py:48
  7.2 2.5 collective-permute-start
  10.5 5.9 collective-permute-start.1
  16.5 4.2 collective-permute-start.2
  21.5 59.2 %copy-start.4 = (f32[1024]{0:T(1024)S(1)}, f32[1024]{0:T(1024)}, u32[]{:S(2)}) copy-start(f32[1024]{0:T(1024)} %param.8) | copy-start | bytes 12292
  21.5 253.3 %all-reduce.2.cloned.1.call-start = ((), (), s32[]{:S(2)}) async-start(), calls=%async_computation.1 | async-start | bytes 8388608 | tf_op jit(solution)/shard_map/psum | solution.py:54
  79.3 1.3 copy-start.5
  90.1 262.1 %all-gather.8.cloned.1.call-start = ((), (), s32[]{:S(2)}) async-start(), calls=%async_computation.2 | async-start | bytes 8912896 | tf_op jit(solution)/shard_map/all_gather | solution.py:56
  276.7 392.6 %all-gather.10.cloned.1.call-start = ((), (), s32[]{:S(2)}) async-start(), calls=%async_computation.3 | async-start | bytes 4227072 | tf_op jit(solution)/shard_map/all_gather | solution.py:74
  276.8 88.4 %copy-start.2 = (bf16[64,256]{1,0:T(8,128)(2,1)S(1)}, bf16[64,256]{1,0:T(8,128)(2,1)}, u32[]{:S(2)}) copy-start(bf16[64,256]{1,0:T(8,128)(2,1)} %param.6) | copy-start | bytes 98308
  365.9 306.2 %copy-start.1 = (f32[64,256]{1,0:T(8,128)}, f32[64,256]{1,0:T(8,128)S(1)}, u32[]{:S(2)}) copy-start(f32[64,256]{1,0:T(8,128)S(1)} %get-tuple-element.13) | copy-start | bytes 196612
  683.9 12.7 %slice-start = ((s8[8388608]{0:T(1024)(128)(4,1)}), s8[4194304]{0:T(1024)(128)(4,1)S(1)}, s32[]{:S(2)}) async-start(s8[8388608]{0:T(1024)(128)(4,1)} %bitcast.31), calls=%async_computation.4 | async-start | bytes 8388608
  685.3 11.2 %copy-start = (bf16[2,512,2048]{2,1,0:T(8,128)(2,1)S(1)}, bf16[2,512,2048]{2,1,0:T(8,128)(2,1)}, u32[]{:S(2)}) copy-start(bf16[2,512,2048]{2,1,0:T(8,128)(2,1)} %constant_dynamic-update-slice_fusion) | copy-start | bytes 12582916
  685.3 11.2 %slice-start.1 = ((s8[8388608]{0:T(1024)(128)(4,1)}), s8[4194304]{0:T(1024)(128)(4,1)S(1)}, s32[]{:S(2)}) async-start(s8[8388608]{0:T(1024)(128)(4,1)} %bitcast.31), calls=%async_computation.5 | async-start | bytes 8388608
  685.4 11.2 %copy-start.6 = (f32[512,1024]{1,0:T(8,128)S(1)}, f32[512,1024]{1,0:T(8,128)}, u32[]{:S(2)}) copy-start(f32[512,1024]{1,0:T(8,128)} %copy-done.5) | copy-start | bytes 6291460
  701.8 11.7 %copy-start.3 = (bf16[512,2048]{1,0:T(8,128)(2,1)S(1)}, bf16[512,2048]{1,0:T(8,128)(2,1)}, u32[]{:S(2)}) copy-start(bf16[512,2048]{1,0:T(8,128)(2,1)} %all-gather.6.cloned.1.call-done) | copy-start | bytes 6291460
Sparse Core Ops, SparseCore 0:
  21.6 52.5 all-gather.5
  90.3 184.5 all-reduce.1
  277.9 74.3 all-gather.7
  366.0 303.3 all-gather.9
where the time goes:
time: 726 us
  waiting for transfers between devices  557 us (77%)
  blocking collectives  64.1 us (9%)
  matrix products  35.4 us (5%)
  local copies, waits for them, and re-layouts  24.7 us (3%)
  other arithmetic  22 us (3%)
  between operations  15.7 us (2%)
    all_gather x1, waiting for transfers between devices, on_device(): lax.all_gather(scaled[None], ('layer', 'feat'), axis=0, tiled=True)  238 us
    psum x1, waiting for transfers between devices, on_device(): lax.psum(partial_value.astype(jnp.bfloat16), 'feat').astype(jnp.float32)  185 us
    all_gather x1, waiting for transfers between devices, on_device(): lax.all_gather(summed_rows[None].astype(jnp.bfloat16), 'layer', axis=0, t...  75.4 us
    psum x1, blocking collectives, on_device(): squares = lax.psum(jnp.sum(recon_error * recon_error), ('layer', 'feat'))  64.1 us
    all_gather x1, waiting for transfers between devices, on_device(): inputs = lax.all_gather(joined, 'feat', axis=0, tiled=True)  52.6 us
    unnamed x20, local copies, waits for them, and re-layouts  14.6 us
  transfers between devices with their start and end apart: 7, of which 7 were waited for; matrix products, arithmetic and copies ran while one was open for 0% of the time, Pallas kernels for 0%

commit v1 on v0

--- a/solution.py
+++ b/solution.py
@@ -7,6 +7,13 @@
 LAYERS = 2
 TOK = 512
 loss_scale = 64.0
+
+
+def perform_sheets(array_in):
+    odd = jnp.stack([array_in] * lax.axis_size(("layer", "feat")), 0)
+    taken_in = lax.all_to_all(odd, ("layer", "feat"), 0, 0)
+    kept_arr = jnp.concatenate(taken_in, 0)
+    return kept_arr
 
 
 def swapped(value, axis, stride):
@@ -71,7 +78,7 @@
     squares = lax.psum(jnp.sum(recon_error * recon_error), ("layer", "feat"))
     mean_square = squares / (LAYERS * TOK * D)
     scaled = (loss_scale / TOK * recon_error).astype(jnp.bfloat16)
-    gathered = lax.all_gather(scaled[None], ("layer", "feat"), axis=0, tiled=True)
+    gathered = perform_sheets(scaled[None])
     own_grad = arrange_group(gathered, layer_group, feat_count, sub_count)
     next_index = jnp.minimum(layer_group + 1, LAYERS - 1)
     next_grad = arrange_group(gathered, next_index, feat_count, sub_count)

time: 726 us -> 540 us (0.74)
  waiting for transfers between devices: 557 us -> 319 us
  blocking collectives: 64.1 us -> 105 us
  local copies, waits for them, and re-layouts: 24.7 us -> 32.5 us
    all_gather x1 -> x0, waiting for transfers between devices: 238 us -> none  [on_device(): lax.all_gather(scaled[None], ('layer', 'feat'), axis=0, tiled=True)]
    psum x1, blocking collectives: 64.1 us -> 105 us  [on_device(): squares = lax.psum(jnp.sum(recon_error * recon_error), ('layer', 'feat'))]
  transfers between devices with their start and end apart: 7 -> 7, of which waited for: 7 -> 6; matrix products, arithmetic and copies ran while one was open for 0% -> 0% of each run, Pallas kernels for 0% -> 0%
where the time goes in v1:
time: 540 us; the launch traced here: 539 us
  waiting for transfers between devices  319 us (59%)
  blocking collectives  105 us (19%)
  matrix products  35.4 us (7%)
  local copies, waits for them, and re-layouts  32.5 us (6%)
  other arithmetic  19.6 us (4%)
  between operations  15.7 us (3%)
  starting transfers between devices  12.7 us (2%)
    psum x1, waiting for transfers between devices, on_device(): lax.psum(partial_value.astype(jnp.bfloat16), 'feat').astype(jnp.float32)  185 us
    psum x1, blocking collectives, on_device(): squares = lax.psum(jnp.sum(recon_error * recon_error), ('layer', 'feat'))  105 us
    all_gather x1, waiting for transfers between devices, on_device(): lax.all_gather(summed_rows[None].astype(jnp.bfloat16), 'layer', axis=0, t...  75.4 us
    all_gather x1, waiting for transfers between devices, on_device(): inputs = lax.all_gather(joined, 'feat', axis=0, tiled=True)  52.6 us
    unnamed x20, local copies, waits for them, and re-layouts  16.3 us
    convert_element_type x1, other arithmetic, on_device(): gathered = lax.all_gather(summed_rows[None].astype(jnp.bfloat16), 'layer'...  11.3 us
    dot_general x1, matrix products, on_device(): jnp.einsum('tf,ktd->kfd', features, recon_grads, preferred_element_type=j...  11.2 us
  transfers between devices with their start and end apart: 7, of which 6 were waited for; matrix products, arithmetic and copies ran while one was open for 0% of the time, Pallas kernels for 0%

profile of v1, /device:TPU:1, one launch (start us, length us, event | category | flops | bytes accessed | tf_op | source)
XLA Modules:
  0.0 539.3 jit_solution(2553826560692465514)
XLA Ops:
  7.2 0.0 all-gather.4.cloned.1.call-start
  7.2 1.5 collective-permute-start
  8.7 1.1 collective-permute-done
  9.7 0.8 broadcast_select_fusion.5
  10.5 3.8 collective-permute-start.1
  14.3 2.1 collective-permute-done.1
  16.5 1.4 collective-permute-start.2
  17.9 2.8 collective-permute-done.2
  20.7 0.7 pad_maximum_fusion
  21.5 0.0 all-gather.4.cloned.1.call-update
  21.5 0.0 copy-start.4
  21.5 0.0 all-reduce.2.cloned.1.call-start
  21.5 52.6 %all-gather.4.cloned.1.call-done = bf16[512,2048]{1,0:T(8,128)(2,1)} async-done(((bf16[64,2048]{1,0:T(8,128)(2,1)}), bf16[512,2048]{1,0:T(8,128)(2,1)}) %all-gather.4.cloned.1.call-update) | async-done | bytes 2097168 | tf_op jit(solution)/shard_map/all_gather | solution.py:55
  74.2 5.1 fusion.6
  79.3 0.0 copy-start.5
  79.3 1.3 copy-done.5
  80.7 0.0 copy-done.4
  80.7 9.4 %convolution_convert_fusion = bf16[512,2,2048]{2,0,1:T(8,128)(2,1)} fusion(bf16[2,1024,2048]{2,1,0:T(8,128)(2,1)} %param.9, f32[512,1024]{1,0:T(8,128)S(1)} %fusion.6, f32[1024]{0:T(1024)S(1)} %copy-done.4), kind=kOutput, calls=%fused_computation.1 | convolution fusion | flops 4298637312 | bytes 14684160 | tf_op jit(solution)/shard_map/tf,kfd->tkd/dot_general | solution.py:58
  90.1 0.0 all-reduce.2.cloned.1.call-update
  90.1 0.0 all-gather.6.cloned.1.call-start
  90.2 184.6 %all-reduce.2.cloned.1.call-done = bf16[512,2,2048]{2,0,1:T(8,128)(2,1)} async-done(((bf16[512,2,2048]{2,0,1:T(8,128)(2,1)}), bf16[512,2,2048]{2,0,1:T(8,128)(2,1)}) %all-reduce.2.cloned.1.call-update) | async-done | bytes 4194320 | tf_op jit(solution)/shard_map/psum | solution.py:61
  274.8 1.9 convert_convert_fusion
  276.7 0.0 all-gather.6.cloned.1.call-update
  276.8 0.0 copy-start.2
  276.8 75.4 %all-gather.6.cloned.1.call-done = bf16[1024,2,2048]{2,0,1:T(8,128)(2,1)} async-done(((bf16[64,2,2048]{2,0,1:T(8,128)(2,1)}), bf16[1024,2,2048]{2,0,1:T(8,128)(2,1)}) %all-gather.6.cloned.1.call-update) | async-done | bytes 8388624 | tf_op jit(solution)/shard_map/all_gather | solution.py:63
  352.2 11.3 %bitcast_convert_fusion = f32[16,64,2,2048]{3,1,0,2:T(8,128)} fusion(bf16[1024,2,2048]{2,0,1:T(8,128)(2,1)} %all-gather.6.cloned.1.call-done), kind=kLoop, calls=%fused_computation.27 | loop fusion | flops 4194304 | bytes 25165824 | tf_op jit(solution)/shard_map/convert_element_type | solution.py:65
  363.5 1.7 dynamic-slice_reduce_fusion
  365.2 0.0 copy-done.2
  365.2 0.0 copy-start.1
  365.3 2.5 stack.7
  367.8 5.9 %all-to-all-start = ((bf16[128,1,64,256]{3,2,1,0:T(8,128)(2,1)}), bf16[128,1,64,256]{3,2,1,0:T(8,128)(2,1)}, u32[]{:S(2)}, u32[]{:S(2)}) async-start(bf16[128,1,64,256]{3,2,1,0:T(8,128)(2,1)} %stack.7), calls=%async_computation | async-start | bytes 8388608 | tf_op jit(solution)/shard_map/all_to_all | solution.py:14
  373.8 0.6 multiply_reduce_fusion
  374.4 104.6 %psum.15 = f32[]{:T(128)} all-reduce(f32[]{:T(128)} %multiply_reduce_fusion), channel_id=1, replica_groups=mesh['layer'=16,'feat'=8] {'layer','feat'}, use_global_device_ids=true, to_apply=%region_4.5 | all-reduce | flops 1 | bytes 8 | tf_op jit(solution)/shard_map/psum | solution.py:78
  479.6 0.0 all-to-all-done
  479.6 2.5 select_bitcast_fusion
  482.1 2.6 copy.16
  484.7 4.2 stack_reshape.3
  488.9 3.2 constant_dynamic-update-slice_fusion.1
  492.1 2.6 copy.17
  494.7 2.9 select_n.126
  497.5 0.0 slice-start
  497.5 1.5 constant_dynamic-update-slice_fusion
  499.0 11.2 %convert_bitcast_fusion = bf16[2,1024,2048]{1,2,0:T(8,128)(2,1)} fusion(bf16[2,512,2048]{2,1,0:T(8,128)(2,1)} %constant_dynamic-update-slice_fusion, f32[512,1024]{1,0:T(8,128)} %copy-done.5, f32[1024]{0:T(1024)S(1)} %copy-done.4), kind=kOutput, calls=%fused_computation | convolution fusion | flops 4300734464 | bytes 14684160 | tf_op jit(solution)/shard_map/tf,ktd->kfd/dot_general | solution.py:91
  510.2 0.0 slice-done
  510.2 0.0 slice-done.1
  510.2 5.2 convert_reduce_fusion
  515.5 11.7 %copy.19 = bf16[2,1024,2048]{2,1,0:T(8,128)(2,1)} copy(bf16[2,1024,2048]{1,2,0:T(8,128)(2,1)} %convert_bitcast_fusion) | data formatting | bytes 16777216
  527.2 4.4 convolution_convert_fusion.1
  (14 shorter events, 0.1 us)
Async XLA Ops:
  7.2 67.0 %all-gather.4.cloned.1.call-start = ((), (), s32[]{:S(2)}) async-start(), calls=%async_computation.1 | async-start | bytes 2359296 | tf_op jit(solution)/shard_map/all_gather | solution.py:55
  7.2 2.5 collective-permute-start
  10.5 5.9 %collective-permute-start.1 = (bf16[64,512]{1,0:T(8,128)(2,1)S(1)}, bf16[64,512]{1,0:T(8,128)(2,1)S(1)}, u32[]{:S(2)}, u32[]{:S(2)}) collective-permute-start(bf16[64,512]{1,0:T(8,128)(2,1)S(1)} %pad_maximum_fusion.2), channel_id=1, source_target_pairs={{0,16},{8,24},{16,0},{24,8},{32,48},{40,56},{48,32},{56,40},{64,80... | collective-permute-start | bytes 196616 | tf_op jit(solution)/shard_map/ppermute | solution.py:22
  16.5 4.2 collective-permute-start.2
  21.5 59.2 %copy-start.4 = (f32[1024]{0:T(1024)S(1)}, f32[1024]{0:T(1024)}, u32[]{:S(2)}) copy-start(f32[1024]{0:T(1024)} %param.8) | copy-start | bytes 12292
  21.5 253.3 %all-reduce.2.cloned.1.call-start = ((), (), s32[]{:S(2)}) async-start(), calls=%async_computation.2 | async-start | bytes 8388608 | tf_op jit(solution)/shard_map/psum | solution.py:61
  79.3 1.3 copy-start.5
  90.1 262.1 %all-gather.6.cloned.1.call-start = ((), (), s32[]{:S(2)}) async-start(), calls=%async_computation.3 | async-start | bytes 8912896 | tf_op jit(solution)/shard_map/all_gather | solution.py:63
  276.8 88.4 %copy-start.2 = (bf16[64,256]{1,0:T(8,128)(2,1)S(1)}, bf16[64,256]{1,0:T(8,128)(2,1)}, u32[]{:S(2)}) copy-start(bf16[64,256]{1,0:T(8,128)(2,1)} %param.6) | copy-start | bytes 98308
  365.2 8.5 %copy-start.1 = (f32[64,256]{1,0:T(8,128)}, f32[64,256]{1,0:T(8,128)S(1)}, u32[]{:S(2)}) copy-start(f32[64,256]{1,0:T(8,128)S(1)} %get-tuple-element.23) | copy-start | bytes 196612
  367.8 111.8 %all-to-all-start = ((bf16[128,1,64,256]{3,2,1,0:T(8,128)(2,1)}), bf16[128,1,64,256]{3,2,1,0:T(8,128)(2,1)}, u32[]{:S(2)}, u32[]{:S(2)}) async-start(bf16[128,1,64,256]{3,2,1,0:T(8,128)(2,1)} %stack.7), calls=%async_computation | async-start | bytes 8388608 | tf_op jit(solution)/shard_map/all_to_all | solution.py:14
  497.5 12.7 %slice-start = ((s8[8388608]{0:T(1024)(128)(4,1)}), s8[4194304]{0:T(1024)(128)(4,1)S(1)}, s32[]{:S(2)}) async-start(s8[8388608]{0:T(1024)(128)(4,1)} %bitcast.30), calls=%async_computation.4 | async-start | bytes 8388608
  499.0 11.2 %copy-start = (bf16[2,512,2048]{2,1,0:T(8,128)(2,1)S(1)}, bf16[2,512,2048]{2,1,0:T(8,128)(2,1)}, u32[]{:S(2)}) copy-start(bf16[2,512,2048]{2,1,0:T(8,128)(2,1)} %constant_dynamic-update-slice_fusion) | copy-start | bytes 12582916
  499.0 11.2 %slice-start.1 = ((s8[8388608]{0:T(1024)(128)(4,1)}), s8[4194304]{0:T(1024)(128)(4,1)S(1)}, s32[]{:S(2)}) async-start(s8[8388608]{0:T(1024)(128)(4,1)} %bitcast.30), calls=%async_computation.5 | async-start | bytes 8388608
  499.0 11.2 %copy-start.6 = (f32[512,1024]{1,0:T(8,128)S(1)}, f32[512,1024]{1,0:T(8,128)}, u32[]{:S(2)}) copy-start(f32[512,1024]{1,0:T(8,128)} %copy-done.5) | copy-start | bytes 6291460
  515.5 11.7 %copy-start.3 = (bf16[512,2048]{1,0:T(8,128)(2,1)S(1)}, bf16[512,2048]{1,0:T(8,128)(2,1)}, u32[]{:S(2)}) copy-start(bf16[512,2048]{1,0:T(8,128)(2,1)} %all-gather.4.cloned.1.call-done) | copy-start | bytes 6291460
Sparse Core Ops, SparseCore 0:
  21.6 52.5 all-gather.3
  90.2 184.5 all-reduce.1
  277.9 74.3 all-gather.5
